TPU v7x, 32 devices: a whole 2x2x4 slice. The times are simulated.
32 devices in a mesh: ens: 8 (over y, x, core), lon: 4 (over z).
Axes of the slice: x: 2, y: 2, z: 4, core: 2. Of those that a mesh axis runs over, the one named last changes fastest.
Arguments:
- features: bfloat16 [8, 384, 46080], P('ens', None, 'lon'), may hold values from -6 to 6
- proj_weight: bfloat16 [648, 384], replicated, may hold values from -0.3125 to 0.3125
- basis_vals: float32 [32, 32, 9], replicated, may hold values from -0.375 to 0.375
- row_of: int32 [32, 32], replicated, may hold values from 0 to 31
- col_off: int32 [32, 32], replicated, may hold values from -4 to 4
- observed: float32 [72, 46080], P(None, 'lon'), may hold values from -6 to 6
- lat_weight: float32 [32], replicated, may hold values from 0.3 to 1
Outputs:
- feature_grad: bfloat16 [8, 384, 46080], P('ens', None, 'lon')
- weight_grad: float32 [648, 384], replicated
Inputs may be any that keep to these rules, and one draw needn't show every extreme that they name: row_of names a row of the slab. col_off is a longitude offset in columns.
All inputs are finite; a program needn't handle non-finite values.
Results may differ from a plain program's by a relative error of at most 0.0089.
Values may be sent and summed in bfloat16 or wider, within the bound.
A program may use at most 256 MiB of HBM per device.

v0:
```python
import math
import jax
import jax.numpy as jnp
from jax import lax
from jax.sharding import PartitionSpec as P

O = 72
K = 9
R = 4
LAT = 32
SMOOTH = 0.25


def extended(cells, sides, width):
    for axis, dim in sides:
        count = lax.axis_size(axis)
        head = lax.slice_in_dim(cells, 0, width, axis=dim)
        tail = lax.slice_in_dim(cells, cells.shape[dim] - width, cells.shape[dim], axis=dim)
        cells = jnp.concatenate(
            [
                lax.ppermute(tail, axis, [(i, (i + 1) % count) for i in range(count)]),
                cells,
                lax.ppermute(head, axis, [((i + 1) % count, i) for i in range(count)]),
            ],
            axis=dim,
        )
    return cells


def passed_along(value, axis, steps):
    count = lax.axis_size(axis)
    pairs = [(source, (source + steps) % count) for source in range(count)]
    return lax.ppermute(value, axis, pairs)


def kernel_table(basis_vals, row_of, col_off):
    offsets = jnp.arange(2 * R + 1, dtype=jnp.int32) - R
    row_ids = jnp.arange(LAT, dtype=jnp.int32)
    row_hit = (row_of[:, :, None] == row_ids[None, None, :]).astype(jnp.float32)
    col_hit = (col_off[:, :, None] == offsets[None, None, :]).astype(jnp.float32)
    kernel = jnp.einsum(
        "isk,isr,isd->dkir", basis_vals, row_hit, col_hit, precision=lax.Precision.HIGHEST
    )
    return kernel.astype(jnp.bfloat16)


def smooth_slope(diff):
    return diff / jnp.sqrt(diff * diff + SMOOTH * SMOOTH)


def pair_spread(values, others):

    def add_member(index, total):
        single = lax.dynamic_index_in_dim(others, index, 0, keepdims=True)
        return total + smooth_slope(values - single)

    return lax.fori_loop(0, others.shape[0], add_member, jnp.zeros(values.shape, jnp.float32))


def shards(features, proj_weight, basis_vals, row_of, col_off, observed, lat_weight):
    mem_dev = features.shape[0]
    chan_in = features.shape[1]
    cell_count = features.shape[2]
    lon_dev = cell_count // LAT
    rim_cells = R * LAT
    span = lon_dev * O
    kernel = kernel_table(basis_vals, row_of, col_off)
    weight_three = proj_weight.reshape(K, O, chan_in)
    widened = extended(features, (("lon", 2),), rim_cells)
    widened = widened.reshape(mem_dev, chan_in, lon_dev + 2 * R, LAT)
    projected = jnp.einsum(
        "koc,mcjr->mkrjo", weight_three, widened, preferred_element_type=jnp.float32
    ).astype(jnp.bfloat16)
    projected = projected.reshape(mem_dev, K, LAT, (lon_dev + 2 * R) * O)
    decoded = jnp.zeros((mem_dev, LAT, span), jnp.float32)
    for offset in range(2 * R + 1):
        window = projected[:, :, :, offset * O : offset * O + span]
        decoded = decoded + jnp.einsum(
            "kir,mkrx->mix", kernel[offset], window, preferred_element_type=jnp.float32
        )
    flat_out = decoded.reshape(mem_dev, LAT * span)
    observed_flat = observed.reshape(O, lon_dev, LAT).transpose(2, 1, 0).reshape(LAT * span)
    everyone = lax.all_gather(flat_out, "ens", axis=0, tiled=True)
    total_count = everyone.shape[0]
    spread = pair_spread(flat_out, everyone)
    slopes = smooth_slope(flat_out - observed_flat[None, :]) - spread / (total_count - 1)
    cotangent = (slopes.reshape(mem_dev, LAT, span) * lat_weight[None, :, None]).astype(
        jnp.bfloat16
    )
    padded = jnp.pad(cotangent, ((0, 0), (0, 0), (2 * R * O, 2 * R * O)))
    ext_len = (lon_dev + 2 * R) * O
    stacked = jnp.stack(
        [
            padded[:, :, (2 * R - offset) * O : (2 * R - offset) * O + ext_len]
            for offset in range(2 * R + 1)
        ]
    )
    spread_wide = jnp.einsum("dkir,dmix->mkrx", kernel, stacked, preferred_element_type=jnp.float32)
    left_part = spread_wide[:, :, :, : R * O]
    right_part = spread_wide[:, :, :, (lon_dev + R) * O :]
    from_left = passed_along(right_part.astype(jnp.bfloat16), "lon", 1).astype(right_part.dtype)
    from_right = passed_along(left_part.astype(jnp.bfloat16), "lon", -1).astype(left_part.dtype)
    interior = spread_wide[:, :, :, R * O : (lon_dev + R) * O]
    interior = interior.at[:, :, :, : R * O].add(from_left)
    interior = interior.at[:, :, :, span - R * O :].add(from_right)
    grad_local = interior.astype(jnp.bfloat16).reshape(mem_dev, K, LAT, lon_dev, O)
    feature_grad = jnp.einsum(
        "koc,mkrjo->mcjr", weight_three, grad_local, preferred_element_type=jnp.float32
    ).astype(jnp.bfloat16)
    feature_grad = feature_grad.reshape(mem_dev, chan_in, cell_count)
    feature_cells = features.reshape(mem_dev, chan_in, lon_dev, LAT)
    weight_part = jnp.einsum(
        "mkrjo,mcjr->koc", grad_local, feature_cells, preferred_element_type=jnp.float32
    ).reshape(K * O, chan_in)
    members_all = mem_dev * lax.axis_size("ens")
    columns_all = lon_dev * lax.axis_size("lon")
    weight_grad = lax.psum(weight_part, ("ens", "lon")) / math.sqrt(members_all * columns_all * LAT)
    return (feature_grad, weight_grad)


def solution(mesh):
    in_specs = (P("ens", None, "lon"), P(), P(), P(), P(), P(None, "lon"), P())
    out_specs = (P("ens", None, "lon"), P())
    return jax.shard_map(shards, mesh=mesh, in_specs=in_specs, out_specs=out_specs, check_vma=False)
```

profile of v0, /device:TPU:0, one launch (start us, length us, event | category | flops | bytes accessed | tf_op | source)
XLA Modules:
  0.0 897.1 jit_solution(3145240483996057671)
XLA Ops:
  8.2 3.1 collective-permute-start
  11.3 2.1 collective-permute-start.1
  15.2 2.1 fusion.17
  19.3 7.4 pad_maximum_fusion
  26.8 12.0 %copy.94 = bf16[1,384,11776]{1,2,0:T(8,128)(2,1)} copy(bf16[1,384,11776]{2,1,0:T(8,128)(2,1)} %pad_maximum_fusion) | data formatting | bytes 18087936 | tf_op jit(solution)/shard_map/concatenate | solution.py:19
  38.8 24.2 %convert_bitcast_fusion = bf16[1,9,32,368,72]{4,2,1,3,0:T(8,128)(2,1)} fusion(bf16[384,368,32,1]{0,2,3,1:T(8,128)(2,1)} %bitcast.191, bf16[9,72,384,1]{2,1,0,3:T(8,128)(2,1)S(1)} %bitcast.183), kind=kOutput, calls=%fused_computation.21 | convolution fusion | flops 5868122112 | bytes 24803328 | tf_op jit(solution)/shard_map/koc,mcjr->mkrjo/dot_general | solution.py:71
  63.0 23.9 %copy.95 = bf16[1,9,32,368,72]{4,3,2,1,0:T(8,128)(2,1)} copy(bf16[1,9,32,368,72]{4,2,1,3,0:T(8,128)(2,1)} %convert_bitcast_fusion) | data formatting | bytes 30523392 | tf_op jit(solution)/shard_map/convert_element_type | solution.py:73
  86.9 39.8 %reshape.238 = bf16[1,9,32,26496]{3,2,1,0:T(8,128)(2,1)} reshape(bf16[1,9,32,368,72]{4,3,2,1,0:T(8,128)(2,1)} %copy.95) | data formatting | bytes 30523392 | tf_op jit(solution)/shard_map/reshape | solution.py:74
  126.7 8.4 convolution_bitcast_fusion.6
  135.1 1.3 copy-done.1
  136.4 6.0 convolution_bitcast_fusion.7
  142.3 7.7 convolution_bitcast_fusion.8
  150.1 7.9 convolution_bitcast_fusion.3
  158.0 7.8 convolution_bitcast_fusion.4
  165.8 8.2 convolution_bitcast_fusion.1
  173.9 9.3 %fusion.3 = f32[25920,32]{0,1:T(8,128)S(1)} fusion(f32[25920,32]{0,1:T(8,128)S(1)} %convolution_bitcast_fusion.6, f32[25920,32]{0,1:T(8,128)S(1)} %convolution_bitcast_fusion.7, f32[25920,32]{0,1:T(8,128)} %convolution_bitcast_fusion.8, bf16[1,9,32,26496]{3,2,1,0:T(8,128)(2,1)} %reshape.238, bf16[9,32,32]{2,0,1:T(8,128)(2,1)} %get-tuple-element.147), kind=kOutput, calls=%fused_computation.14 | convolution fusion | flops 480245760 | bytes 28377088 | tf_op jit(solution)/shard_map/kir,mkrx->mix/dot_general | solution.py:78
  183.3 12.7 %fusion.6 = f32[25920,32]{0,1:T(8,128)S(1)} fusion(f32[25920,32]{0,1:T(8,128)} %convolution_bitcast_fusion.3, f32[25920,32]{0,1:T(8,128)} %convolution_bitcast_fusion.4, f32[25920,32]{0,1:T(8,128)S(1)} %fusion.3, bf16[1,9,32,26496]{3,2,1,0:T(8,128)(2,1)} %reshape.238, bf16[9,32,32]{2,0,1:T(8,128)(2,1)S(1)} %get-tuple-element.143), kind=kOutput, calls=%fused_computation.17 | convolution fusion | flops 480245760 | bytes 28272640 | tf_op jit(solution)/shard_map/kir,mkrx->mix/dot_general | solution.py:78
  196.0 12.1 %fusion.9 = f32[1,32,25920]{2,1,0:T(8,128)} fusion(f32[25920,32]{0,1:T(8,128)S(1)} %copy-done.6, f32[25920,32]{0,1:T(8,128)S(1)} %fusion.6, bf16[1,9,32,26496]{3,2,1,0:T(8,128)(2,1)} %reshape.238, bf16[9,32,32]{2,0,1:T(8,128)(2,1)S(1)} %copy-done.4), kind=kOutput, calls=%fused_computation.20 | convolution fusion | flops 479416320 | bytes 24938496 | tf_op jit(solution)/shard_map/kir,mkrx->mix/dot_general | solution.py:78
  208.1 7.5 reshape.260
  215.6 5.7 copy.106
  221.3 9.9 %copy.107 = f32[32,360,72]{2,1,0:T(8,128)} copy(f32[32,360,72]{2,0,1:T(8,128)} %bitcast.190) | data formatting | bytes 6635520 | tf_op jit(solution)/shard_map/transpose | solution.py:82
  231.2 12.0 %broadcast_in_dim_reshape.3 = f32[1,829440]{1,0:T(1,128)} reshape(f32[32,360,72]{2,1,0:T(8,128)} %copy.107) | data formatting | bytes 6635520 | tf_op jit(solution)/shard_map/broadcast_in_dim;reshape | solution.py:86
  243.2 7.9 reshape.248
  251.1 95.3 %all-gather.3.cloned.1.call-done = f32[8,1,829440]{2,1,0:T(1,128)} async-done(((f32[1,1,829440]{2,1,0:T(1,128)}), f32[8,1,829440]{2,1,0:T(1,128)}) %all-gather.3.cloned.1.call-update) | async-done | bytes 26542096 | tf_op jit(solution)/shard_map/all_gather | solution.py:83
  346.4 22.3 %copy.152 = f32[8,1,829440]{2,0,1:T(8,128)} copy(f32[8,1,829440]{2,1,0:T(1,128)} %all-gather.3.cloned.1.call-done) | data formatting | bytes 53084160
  368.7 126.8 %while.16 = (s32[]{:T(128)}, f32[1,829440]{1,0:T(1,128)}, f32[8,829440]{1,0:T(8,128)}, f32[1,829440]{1,0:T(1,128)}, s32[]{:T(128)}, /*index=5*/s32[]{:T(128)}) while((s32[]{:T(128)}, f32[1,829440]{1,0:T(1,128)}, f32[8,829440]{1,0:T(8,128)}, f32[1,829440]{1,0:T(1,128)}, s32[]{:T(128)}, /*index=5*/s32[]{:T(128)}) %tuple.65), condition=%wide.region_1.2_spmd.clone, body=%wide.region_0.1_spmd.clone.sunk | while | flops 4976643 | bytes 13271123 | solution.py:57
  368.7 15.1 %fusion.45 = f32[1,829440]{1,0:T(1,128)} fusion(f32[1,829440]{1,0:T(1,128)} %get-tuple-element.182, pred[]{:T(512)S(6)} %compare.15, f32[1,829440]{1,0:T(1,128)} %get-tuple-element.190, f32[8,829440]{1,0:T(8,128)} %get-tuple-element.189, s32[]{:T(128)} %get-tuple-element.181), kind=kLoop, calls=%fused_computation.1.clone.1 | loop fusion | flops 4976640 | bytes 13271045 | tf_op jit(solution)/shard_map/while/body/eval_jaxpr/add | solution.py:55
  383.8 16.0 %fusion.45 = f32[1,829440]{1,0:T(1,128)} fusion(f32[1,829440]{1,0:T(1,128)} %get-tuple-element.182, pred[]{:T(512)S(6)} %compare.15, f32[1,829440]{1,0:T(1,128)} %get-tuple-element.190, f32[8,829440]{1,0:T(8,128)} %get-tuple-element.189, s32[]{:T(128)} %get-tuple-element.181), kind=kLoop, calls=%fused_computation.1.clone.1 | loop fusion | flops 4976640 | bytes 13271045 | tf_op jit(solution)/shard_map/while/body/eval_jaxpr/add | solution.py:55
  399.7 16.0 %fusion.45 = f32[1,829440]{1,0:T(1,128)} fusion(f32[1,829440]{1,0:T(1,128)} %get-tuple-element.182, pred[]{:T(512)S(6)} %compare.15, f32[1,829440]{1,0:T(1,128)} %get-tuple-element.190, f32[8,829440]{1,0:T(8,128)} %get-tuple-element.189, s32[]{:T(128)} %get-tuple-element.181), kind=kLoop, calls=%fused_computation.1.clone.1 | loop fusion | flops 4976640 | bytes 13271045 | tf_op jit(solution)/shard_map/while/body/eval_jaxpr/add | solution.py:55
  415.7 16.0 %fusion.45 = f32[1,829440]{1,0:T(1,128)} fusion(f32[1,829440]{1,0:T(1,128)} %get-tuple-element.182, pred[]{:T(512)S(6)} %compare.15, f32[1,829440]{1,0:T(1,128)} %get-tuple-element.190, f32[8,829440]{1,0:T(8,128)} %get-tuple-element.189, s32[]{:T(128)} %get-tuple-element.181), kind=kLoop, calls=%fused_computation.1.clone.1 | loop fusion | flops 4976640 | bytes 13271045 | tf_op jit(solution)/shard_map/while/body/eval_jaxpr/add | solution.py:55
  431.6 16.0 %fusion.45 = f32[1,829440]{1,0:T(1,128)} fusion(f32[1,829440]{1,0:T(1,128)} %get-tuple-element.182, pred[]{:T(512)S(6)} %compare.15, f32[1,829440]{1,0:T(1,128)} %get-tuple-element.190, f32[8,829440]{1,0:T(8,128)} %get-tuple-element.189, s32[]{:T(128)} %get-tuple-element.181), kind=kLoop, calls=%fused_computation.1.clone.1 | loop fusion | flops 4976640 | bytes 13271045 | tf_op jit(solution)/shard_map/while/body/eval_jaxpr/add | solution.py:55
  447.6 16.0 %fusion.45 = f32[1,829440]{1,0:T(1,128)} fusion(f32[1,829440]{1,0:T(1,128)} %get-tuple-element.182, pred[]{:T(512)S(6)} %compare.15, f32[1,829440]{1,0:T(1,128)} %get-tuple-element.190, f32[8,829440]{1,0:T(8,128)} %get-tuple-element.189, s32[]{:T(128)} %get-tuple-element.181), kind=kLoop, calls=%fused_computation.1.clone.1 | loop fusion | flops 4976640 | bytes 13271045 | tf_op jit(solution)/shard_map/while/body/eval_jaxpr/add | solution.py:55
  463.5 16.0 %fusion.45 = f32[1,829440]{1,0:T(1,128)} fusion(f32[1,829440]{1,0:T(1,128)} %get-tuple-element.182, pred[]{:T(512)S(6)} %compare.15, f32[1,829440]{1,0:T(1,128)} %get-tuple-element.190, f32[8,829440]{1,0:T(8,128)} %get-tuple-element.189, s32[]{:T(128)} %get-tuple-element.181), kind=kLoop, calls=%fused_computation.1.clone.1 | loop fusion | flops 4976640 | bytes 13271045 | tf_op jit(solution)/shard_map/while/body/eval_jaxpr/add | solution.py:55
  479.5 16.0 %fusion.45 = f32[1,829440]{1,0:T(1,128)} fusion(f32[1,829440]{1,0:T(1,128)} %get-tuple-element.182, pred[]{:T(512)S(6)} %compare.15, f32[1,829440]{1,0:T(1,128)} %get-tuple-element.190, f32[8,829440]{1,0:T(8,128)} %get-tuple-element.189, s32[]{:T(128)} %get-tuple-element.181), kind=kLoop, calls=%fused_computation.1.clone.1 | loop fusion | flops 4976640 | bytes 13271045 | tf_op jit(solution)/shard_map/while/body/eval_jaxpr/add | solution.py:55
  495.4 37.4 %subtract_reduce_fusion = f32[829440]{0:T(1024)} fusion(f32[1,829440]{1,0:T(1,128)} %get-tuple-element.105, f32[1,829440]{1,0:T(1,128)} %get-tuple-element.195, f32[1,829440]{1,0:T(1,128)} %broadcast_in_dim_reshape.3), kind=kLoop, calls=%fused_computation.37 | loop fusion | flops 4976640 | bytes 13271040 | tf_op jit(solution)/shard_map/sub | solution.py:86
  532.8 3.9 reshape.250
  536.7 2.2 multiply_convert_fusion
  539.0 1.3 bitcast_dynamic-update-slice_fusion.7
  540.3 1.7 bitcast_dynamic-update-slice_fusion.6
  542.0 1.7 bitcast_dynamic-update-slice_fusion.5
  543.7 1.7 bitcast_dynamic-update-slice_fusion.4
  545.4 1.7 bitcast_dynamic-update-slice_fusion.3
  547.1 1.7 bitcast_dynamic-update-slice_fusion.2
  548.8 1.7 bitcast_dynamic-update-slice_fusion.1
  550.5 1.8 bitcast_dynamic-update-slice_fusion
  552.3 1.7 bitcast_dynamic-update-slice_fusion.8
  554.0 23.7 %fusion.37 = (bf16[1,9,32,26496]{3,2,1,0:T(8,128)(2,1)}, f32[1,9,32,26496]{3,2,1,0:T(8,128)}) fusion(bf16[9,9,32,32]{3,1,0,2:T(8,128)(2,1)S(1)} %copy-done.3, bf16[9,1,32,26496]{3,2,0,1:T(8,128)(2,1)} %bitcast_dynamic-update-slice_fusion.8), kind=kOutput, calls=%fused_computation.83 | convolution fusion | flops 4402999296 | bytes 61212672 | tf_op jit(solution)/shard_map/dkir,dmix->mkrx/dot_general | solution.py:98
  578.9 1.5 collective-permute-start.2
  580.4 12.4 %copy.120 = bf16[1,384,11520]{1,2,0:T(8,128)(2,1)} copy(bf16[1,384,11520]{2,1,0:T(8,128)(2,1)} %param.13) | data formatting | bytes 17694720 | tf_op args[0]
  592.8 24.6 %slice.209 = f32[1,9,32,25920]{3,2,1,0:T(8,128)} slice(f32[1,9,32,26496]{3,2,1,0:T(8,128)} %get-tuple-element.149), slice={[0:1], [0:9], [0:32], [288:26208]} | slice | bytes 59719680 | tf_op jit(solution)/shard_map/slice | solution.py:103
  617.4 2.3 collective-permute-start.3
  619.7 1.2 slice_add_fusion.1
  621.0 3.7 scatter-add.6
  625.9 3.6 scatter-add.9
  629.5 16.5 %convert_element_type.58 = bf16[1,9,32,25920]{3,2,1,0:T(8,128)(2,1)} convert(f32[1,9,32,25920]{3,2,1,0:T(8,128)} %scatter-add.9) | non-fusion elementwise | flops 7464960 | bytes 44789760 | tf_op jit(solution)/shard_map/convert_element_type | solution.py:106
  646.0 39.2 %reshape.252 = bf16[9,32,360,72]{3,2,1,0:T(8,128)(2,1)} reshape(bf16[1,9,32,25920]{3,2,1,0:T(8,128)(2,1)} %convert_element_type.58) | data formatting | bytes 29859840 | tf_op jit(solution)/shard_map/reshape.105
  685.2 31.7 %copy.119 = bf16[9,72,360,32]{2,3,1,0:T(8,128)(2,1)} copy(bf16[9,72,360,32]{1,2,3,0:T(8,128)(2,1)} %bitcast.185) | data formatting | bytes 29859840 | tf_op jit(solution)/shard_map/mkrjo,mcjr->koc/dot_general | solution.py:112
  716.9 26.0 %copy.121 = bf16[648,360,32]{0,2,1:T(8,128)(2,1)} copy(bf16[648,360,32]{1,2,0:T(8,128)(2,1)} %bitcast.187) | data formatting | bytes 29859840 | tf_op jit(solution)/shard_map/mkrjo,mcjr->koc/dot_general | solution.py:112
  742.9 14.1 %convolution_bitcast_fusion.10 = f32[648,384]{1,0:T(8,128)} fusion(bf16[648,360,32]{0,2,1:T(8,128)(2,1)} %copy.121, bf16[384,360,32]{0,2,1:T(8,128)(2,1)} %bitcast.188), kind=kOutput, calls=%fused_computation.51 | convolution fusion | flops 5733089280 | bytes 24772608 | tf_op jit(solution)/shard_map/mkrjo,mcjr->koc/dot_general | solution.py:112
  757.0 17.2 %fusion.11 = bf16[1,384,360,32]{1,2,3,0:T(8,128)(2,1)} fusion(bf16[9,32,360,72]{3,2,1,0:T(8,128)(2,1)} %reshape.252, bf16[9,72,384,1]{2,1,3,0:T(8,128)(2,1)S(1)} %bitcast.184), kind=kOutput, calls=%fused_computation.35 | convolution fusion | flops 5737512960 | bytes 24274944 | tf_op jit(solution)/shard_map/koc,mkrjo->mcjr/dot_general | solution.py:107
  774.2 8.2 copy.118
  782.4 12.4 %copy.122 = bf16[1,384,11520]{2,1,0:T(8,128)(2,1)} copy(bf16[1,384,11520]{1,2,0:T(8,128)(2,1)} %bitcast.189) | data formatting | bytes 17694720
  794.8 93.0 %all-reduce.3.cloned.1.call-done = f32[648,384]{1,0:T(8,128)} async-done(((f32[648,384]{1,0:T(8,128)}), f32[648,384]{1,0:T(8,128)}) %all-reduce.3.cloned.1.call-update) | async-done | bytes 995344 | tf_op jit(solution)/shard_map/psum | solution.py:117
  887.8 2.2 broadcast_multiply_fusion
  (29 shorter events, 7.3 us)
Async XLA Ops:
  7.2 31.6 %copy-start = (bf16[648,384]{1,0:T(8,128)(2,1)S(1)}, bf16[648,384]{1,0:T(8,128)(2,1)}, u32[]{:S(2)}) copy-start(bf16[648,384]{1,0:T(8,128)(2,1)} %param.14) | copy-start | bytes 1492996
  7.2 339.2 %all-gather.3.cloned.1.call-start = ((), (), s32[]{:S(2)}) async-start(), calls=%async_computation.1 | async-start | bytes 29859840 | tf_op jit(solution)/shard_map/all_gather | solution.py:83
  8.2 11.1 %collective-permute-start = (bf16[1,384,128]{2,1,0:T(8,128)(2,1)S(1)}, bf16[1,384,128]{2,1,0:T(8,128)(2,1)S(1)}, u32[]{:S(2)}, u32[]{:S(2)}) collective-permute-start(bf16[1,384,128]{2,1,0:T(8,128)(2,1)S(1)} %get-tuple-element.137), channel_id=1, source_target_pairs={{0,1},{1,2},{2,3},{3,0},{4,5},{5,6},{6,7},{7,4},{8,9},{9,10},{10,1... | collective-permute-start | bytes 294920 | tf_op jit(solution)/shard_map/ppermute | solution.py:21
  11.3 8.0 collective-permute-start.1
  17.4 1.0 copy-start.2
  126.7 9.7 %copy-start.1 = (bf16[1,9,32,26496]{3,2,1,0:T(8,128)(2,1)S(1)}, bf16[1,9,32,26496]{3,2,1,0:T(8,128)(2,1)}, u32[]{:S(2)}) copy-start(bf16[1,9,32,26496]{3,2,1,0:T(8,128)(2,1)} %reshape.238) | copy-start | bytes 45785092
  183.2 12.7 %copy-start.4 = (bf16[9,32,32]{2,0,1:T(8,128)(2,1)S(1)}, bf16[9,32,32]{2,0,1:T(8,128)(2,1)}, u32[]{:S(2)}) copy-start(bf16[9,32,32]{2,0,1:T(8,128)(2,1)} %get-tuple-element.139) | copy-start | bytes 55300
  183.2 12.7 %copy-start.6 = (f32[25920,32]{0,1:T(8,128)S(1)}, f32[25920,32]{0,1:T(8,128)}, u32[]{:S(2)}) copy-start(f32[25920,32]{0,1:T(8,128)} %convolution_bitcast_fusion.1) | copy-start | bytes 9953284
  215.6 672.2 %all-reduce.3.cloned.1.call-start = ((), (), s32[]{:S(2)}) async-start(), calls=%async_computation | async-start | bytes 1990656 | tf_op jit(solution)/shard_map/psum | solution.py:117
  495.4 41.3 %copy-start.5 = (f32[32]{0:T(128)S(1)}, f32[32]{0:T(128)}, u32[]{:S(2)}) copy-start(f32[32]{0:T(128)} %param.19) | copy-start | bytes 388
  545.4 8.6 copy-start.3
  578.9 40.9 %collective-permute-start.2 = (bf16[1,9,32,288]{3,2,1,0:T(8,128)(2,1)S(1)}, bf16[1,9,32,288]{3,2,1,0:T(8,128)(2,1)S(1)}, u32[]{:S(2)}, u32[]{:S(2)}) collective-permute-start(bf16[1,9,32,288]{3,2,1,0:T(8,128)(2,1)S(1)} %get-tuple-element.136), channel_id=1, source_target_pairs={{0,1},{1,2},{2,3},{3,0},{4,5},{5,6},{6,7},{7,4},{8,9},{9,10},{10,1... | collective-permute-start | bytes 497672 | tf_op jit(solution)/shard_map/ppermute | solution.py:33
  617.4 7.3 collective-permute-start.3
Sparse Core Ops, SparseCore 0:
  215.7 130.6 all-gather.2
  757.1 130.6 all-reduce.2
where the time goes:
time: 912 us; the launch traced here: 897 us
  local copies, waits for them, and re-layouts  328 us (36%)
  other arithmetic  196 us (21%)
  waiting for transfers between devices  188 us (21%)
  matrix products  161 us (18%)
  between operations  14.4 us (2%)
  starting transfers between devices  9.15 us (1%)
    add x8, other arithmetic, add_member(): return total + smooth_slope(values - single)  127 us
    all_gather x1, waiting for transfers between devices, shards(): everyone = lax.all_gather(flat_out, 'ens', axis=0, tiled=True)  95.3 us
    psum x1, waiting for transfers between devices, shards(): lax.psum(weight_part, ('ens', 'lon'))  93 us
    dot_general x9, matrix products, shards(): jnp.einsum('kir,mkrx->mix', kernel[offset], window, preferred_element_typ...  80 us
    unnamed x28, local copies, waits for them, and re-layouts  76.9 us
    dot_general x2, local copies, waits for them, and re-layouts, shards(): jnp.einsum('mkrjo,mcjr->koc', grad_local, feature_cells, preferred_elemen...  57.7 us
    reshape x1, local copies, waits for them, and re-layouts, shards(): projected = projected.reshape(mem_dev, K, LAT, (lon_dev + 2 * R) * O)  39.8 us
    another operation x1, local copies, waits for them, and re-layouts  39.2 us
  transfers between devices with their start and end apart: 6, of which 2 were waited for; matrix products, arithmetic and copies ran while one was open for 13% of the time, Pallas kernels for 0%

commit v1 on v0

--- a/solution.py
+++ b/solution.py
@@ -114,7 +114,9 @@
     ).reshape(K * O, chan_in)
     members_all = mem_dev * lax.axis_size("ens")
     columns_all = lon_dev * lax.axis_size("lon")
-    weight_grad = lax.psum(weight_part, ("ens", "lon")) / math.sqrt(members_all * columns_all * LAT)
+    weight_grad = jnp.sum(lax.all_gather(weight_part, ("ens", "lon")), axis=0) / math.sqrt(
+        members_all * columns_all * LAT
+    )
     return (feature_grad, weight_grad)
 
 

time: 912 us -> 978 us (1.072)
  waiting for transfers between devices: 188 us -> 244 us
  other arithmetic: 196 us -> 206 us
    all_gather x0 -> x1, waiting for transfers between devices: none -> 148 us  [shards(): lax.all_gather(weight_part, ('ens', 'lon'))]
    psum x1 -> x0, waiting for transfers between devices: 93 us -> none  [shards(): lax.psum(weight_part, ('ens', 'lon'))]
    dot_general x2 -> x1, local copies, waits for them, and re-layouts: 57.7 us -> 31.7 us  [shards(): jnp.einsum('mkrjo,mcjr->koc', grad_local, feature_cells, preferred_elemen...]
    another operation x1 -> x2, local copies, waits for them, and re-layouts: 39.2 us -> 65.2 us
    reduce_sum x0 -> x1, other arithmetic: none -> 11.7 us  [shards(): jnp.sum(lax.all_gather(weight_part, ('ens', 'lon')), axis=0)]
where the time goes in v1:
time: 978 us; the launch traced here: 964 us
  local copies, waits for them, and re-layouts  328 us (34%)
  waiting for transfers between devices  244 us (25%)
  other arithmetic  206 us (21%)
  matrix products  162 us (17%)
  between operations  14.4 us (1%)
    all_gather x1, waiting for transfers between devices, shards(): lax.all_gather(weight_part, ('ens', 'lon'))  148 us
    add x8, other arithmetic, add_member(): return total + smooth_slope(values - single)  127 us
    all_gather x1, waiting for transfers between devices, shards(): everyone = lax.all_gather(flat_out, 'ens', axis=0, tiled=True)  95.3 us
    dot_general x9, matrix products, shards(): jnp.einsum('kir,mkrx->mix', kernel[offset], window, preferred_element_typ...  80 us
    unnamed x28, local copies, waits for them, and re-layouts  76.9 us
    another operation x2, local copies, waits for them, and re-layouts  65.2 us
    reshape x1, local copies, waits for them, and re-layouts, shards(): projected = projected.reshape(mem_dev, K, LAT, (lon_dev + 2 * R) * O)  39.8 us
    sub x1, other arithmetic, shards(): smooth_slope(flat_out - observed_flat[None, :]) - spread / (total_count - 1)  37.4 us
  transfers between devices with their start and end apart: 6, of which 2 were waited for; matrix products, arithmetic and copies ran while one was open for 13% of the time, Pallas kernels for 0%

profile of v1, /device:TPU:0, one launch (start us, length us, event | category | flops | bytes accessed | tf_op | source)
XLA Modules:
  0.0 963.7 jit_solution(2448673647923147788)
XLA Ops:
  8.2 3.1 collective-permute-start
  11.3 2.1 collective-permute-start.1
  15.2 2.1 fusion.17
  19.3 7.4 pad_maximum_fusion
  26.8 12.0 %copy.94 = bf16[1,384,11776]{1,2,0:T(8,128)(2,1)} copy(bf16[1,384,11776]{2,1,0:T(8,128)(2,1)} %pad_maximum_fusion) | data formatting | bytes 18087936 | tf_op jit(solution)/shard_map/concatenate | solution.py:19
  38.8 24.2 %convert_bitcast_fusion = bf16[1,9,32,368,72]{4,2,1,3,0:T(8,128)(2,1)} fusion(bf16[384,368,32,1]{0,2,3,1:T(8,128)(2,1)} %bitcast.193, bf16[9,72,384,1]{2,1,0,3:T(8,128)(2,1)S(1)} %bitcast.184), kind=kOutput, calls=%fused_computation.21 | convolution fusion | flops 5868122112 | bytes 24803328 | tf_op jit(solution)/shard_map/koc,mcjr->mkrjo/dot_general | solution.py:71
  63.0 23.9 %copy.95 = bf16[1,9,32,368,72]{4,3,2,1,0:T(8,128)(2,1)} copy(bf16[1,9,32,368,72]{4,2,1,3,0:T(8,128)(2,1)} %convert_bitcast_fusion) | data formatting | bytes 30523392 | tf_op jit(solution)/shard_map/convert_element_type | solution.py:73
  86.9 39.8 %reshape.242 = bf16[1,9,32,26496]{3,2,1,0:T(8,128)(2,1)} reshape(bf16[1,9,32,368,72]{4,3,2,1,0:T(8,128)(2,1)} %copy.95) | data formatting | bytes 30523392 | tf_op jit(solution)/shard_map/reshape | solution.py:74
  126.7 8.4 convolution_bitcast_fusion.6
  135.1 1.3 copy-done.1
  136.4 6.0 convolution_bitcast_fusion.7
  142.3 7.7 convolution_bitcast_fusion.8
  150.1 7.9 convolution_bitcast_fusion.3
  158.0 7.8 convolution_bitcast_fusion.4
  165.8 8.2 convolution_bitcast_fusion.1
  173.9 9.3 fusion.3
  183.3 12.7 %fusion.6 = f32[25920,32]{0,1:T(8,128)S(1)} fusion(f32[25920,32]{0,1:T(8,128)} %convolution_bitcast_fusion.3, f32[25920,32]{0,1:T(8,128)} %convolution_bitcast_fusion.4, f32[25920,32]{0,1:T(8,128)S(1)} %fusion.3, bf16[1,9,32,26496]{3,2,1,0:T(8,128)(2,1)} %reshape.242, bf16[9,32,32]{2,0,1:T(8,128)(2,1)S(1)} %get-tuple-element.143), kind=kOutput, calls=%fused_computation.17 | convolution fusion | flops 480245760 | bytes 28272640 | tf_op jit(solution)/shard_map/kir,mkrx->mix/dot_general | solution.py:78
  196.0 12.1 %fusion.9 = f32[1,32,25920]{2,1,0:T(8,128)} fusion(f32[25920,32]{0,1:T(8,128)S(1)} %copy-done.6, f32[25920,32]{0,1:T(8,128)S(1)} %fusion.6, bf16[1,9,32,26496]{3,2,1,0:T(8,128)(2,1)} %reshape.242, bf16[9,32,32]{2,0,1:T(8,128)(2,1)S(1)} %copy-done.4), kind=kOutput, calls=%fused_computation.20 | convolution fusion | flops 479416320 | bytes 24938496 | tf_op jit(solution)/shard_map/kir,mkrx->mix/dot_general | solution.py:78
  208.1 7.5 reshape.266
  215.6 5.7 copy.106
  221.3 9.9 %copy.107 = f32[32,360,72]{2,1,0:T(8,128)} copy(f32[32,360,72]{2,0,1:T(8,128)} %bitcast.192) | data formatting | bytes 6635520 | tf_op jit(solution)/shard_map/transpose | solution.py:82
  231.2 12.0 %broadcast_in_dim_reshape.3 = f32[1,829440]{1,0:T(1,128)} reshape(f32[32,360,72]{2,1,0:T(8,128)} %copy.107) | data formatting | bytes 6635520 | tf_op jit(solution)/shard_map/broadcast_in_dim;reshape | solution.py:86
  243.2 7.9 reshape.252
  251.1 95.3 %all-gather.7.cloned.1.call-done = f32[8,1,829440]{2,1,0:T(1,128)} async-done(((f32[1,1,829440]{2,1,0:T(1,128)}), f32[8,1,829440]{2,1,0:T(1,128)}) %all-gather.7.cloned.1.call-update) | async-done | bytes 26542096 | tf_op jit(solution)/shard_map/all_gather | solution.py:83
  346.4 22.3 %copy.152 = f32[8,1,829440]{2,0,1:T(8,128)} copy(f32[8,1,829440]{2,1,0:T(1,128)} %all-gather.7.cloned.1.call-done) | data formatting | bytes 53084160
  368.7 126.8 %while.16 = (s32[]{:T(128)}, f32[1,829440]{1,0:T(1,128)}, f32[8,829440]{1,0:T(8,128)}, f32[1,829440]{1,0:T(1,128)}, s32[]{:T(128)}, /*index=5*/s32[]{:T(128)}) while((s32[]{:T(128)}, f32[1,829440]{1,0:T(1,128)}, f32[8,829440]{1,0:T(8,128)}, f32[1,829440]{1,0:T(1,128)}, s32[]{:T(128)}, /*index=5*/s32[]{:T(128)}) %tuple.65), condition=%wide.region_1.2_spmd.clone, body=%wide.region_0.1_spmd.clone.sunk | while | flops 4976643 | bytes 13271123 | solution.py:57
  368.7 15.1 %fusion.45 = f32[1,829440]{1,0:T(1,128)} fusion(f32[1,829440]{1,0:T(1,128)} %get-tuple-element.182, pred[]{:T(512)S(6)} %compare.15, f32[1,829440]{1,0:T(1,128)} %get-tuple-element.190, f32[8,829440]{1,0:T(8,128)} %get-tuple-element.189, s32[]{:T(128)} %get-tuple-element.181), kind=kLoop, calls=%fused_computation.1.clone.1 | loop fusion | flops 4976640 | bytes 13271045 | tf_op jit(solution)/shard_map/while/body/eval_jaxpr/add | solution.py:55
  383.8 16.0 %fusion.45 = f32[1,829440]{1,0:T(1,128)} fusion(f32[1,829440]{1,0:T(1,128)} %get-tuple-element.182, pred[]{:T(512)S(6)} %compare.15, f32[1,829440]{1,0:T(1,128)} %get-tuple-element.190, f32[8,829440]{1,0:T(8,128)} %get-tuple-element.189, s32[]{:T(128)} %get-tuple-element.181), kind=kLoop, calls=%fused_computation.1.clone.1 | loop fusion | flops 4976640 | bytes 13271045 | tf_op jit(solution)/shard_map/while/body/eval_jaxpr/add | solution.py:55
  399.7 16.0 %fusion.45 = f32[1,829440]{1,0:T(1,128)} fusion(f32[1,829440]{1,0:T(1,128)} %get-tuple-element.182, pred[]{:T(512)S(6)} %compare.15, f32[1,829440]{1,0:T(1,128)} %get-tuple-element.190, f32[8,829440]{1,0:T(8,128)} %get-tuple-element.189, s32[]{:T(128)} %get-tuple-element.181), kind=kLoop, calls=%fused_computation.1.clone.1 | loop fusion | flops 4976640 | bytes 13271045 | tf_op jit(solution)/shard_map/while/body/eval_jaxpr/add | solution.py:55
  415.7 16.0 %fusion.45 = f32[1,829440]{1,0:T(1,128)} fusion(f32[1,829440]{1,0:T(1,128)} %get-tuple-element.182, pred[]{:T(512)S(6)} %compare.15, f32[1,829440]{1,0:T(1,128)} %get-tuple-element.190, f32[8,829440]{1,0:T(8,128)} %get-tuple-element.189, s32[]{:T(128)} %get-tuple-element.181), kind=kLoop, calls=%fused_computation.1.clone.1 | loop fusion | flops 4976640 | bytes 13271045 | tf_op jit(solution)/shard_map/while/body/eval_jaxpr/add | solution.py:55
  431.6 16.0 %fusion.45 = f32[1,829440]{1,0:T(1,128)} fusion(f32[1,829440]{1,0:T(1,128)} %get-tuple-element.182, pred[]{:T(512)S(6)} %compare.15, f32[1,829440]{1,0:T(1,128)} %get-tuple-element.190, f32[8,829440]{1,0:T(8,128)} %get-tuple-element.189, s32[]{:T(128)} %get-tuple-element.181), kind=kLoop, calls=%fused_computation.1.clone.1 | loop fusion | flops 4976640 | bytes 13271045 | tf_op jit(solution)/shard_map/while/body/eval_jaxpr/add | solution.py:55
  447.6 16.0 %fusion.45 = f32[1,829440]{1,0:T(1,128)} fusion(f32[1,829440]{1,0:T(1,128)} %get-tuple-element.182, pred[]{:T(512)S(6)} %compare.15, f32[1,829440]{1,0:T(1,128)} %get-tuple-element.190, f32[8,829440]{1,0:T(8,128)} %get-tuple-element.189, s32[]{:T(128)} %get-tuple-element.181), kind=kLoop, calls=%fused_computation.1.clone.1 | loop fusion | flops 4976640 | bytes 13271045 | tf_op jit(solution)/shard_map/while/body/eval_jaxpr/add | solution.py:55
  463.5 16.0 %fusion.45 = f32[1,829440]{1,0:T(1,128)} fusion(f32[1,829440]{1,0:T(1,128)} %get-tuple-element.182, pred[]{:T(512)S(6)} %compare.15, f32[1,829440]{1,0:T(1,128)} %get-tuple-element.190, f32[8,829440]{1,0:T(8,128)} %get-tuple-element.189, s32[]{:T(128)} %get-tuple-element.181), kind=kLoop, calls=%fused_computation.1.clone.1 | loop fusion | flops 4976640 | bytes 13271045 | tf_op jit(solution)/shard_map/while/body/eval_jaxpr/add | solution.py:55
  479.5 16.0 %fusion.45 = f32[1,829440]{1,0:T(1,128)} fusion(f32[1,829440]{1,0:T(1,128)} %get-tuple-element.182, pred[]{:T(512)S(6)} %compare.15, f32[1,829440]{1,0:T(1,128)} %get-tuple-element.190, f32[8,829440]{1,0:T(8,128)} %get-tuple-element.189, s32[]{:T(128)} %get-tuple-element.181), kind=kLoop, calls=%fused_computation.1.clone.1 | loop fusion | flops 4976640 | bytes 13271045 | tf_op jit(solution)/shard_map/while/body/eval_jaxpr/add | solution.py:55
  495.4 37.4 %subtract_reduce_fusion = f32[829440]{0:T(1024)} fusion(f32[1,829440]{1,0:T(1,128)} %get-tuple-element.105, f32[1,829440]{1,0:T(1,128)} %get-tuple-element.195, f32[1,829440]{1,0:T(1,128)} %broadcast_in_dim_reshape.3), kind=kLoop, calls=%fused_computation.37 | loop fusion | flops 4976640 | bytes 13271040 | tf_op jit(solution)/shard_map/sub | solution.py:86
  532.8 3.9 reshape.254
  536.7 2.2 multiply_convert_fusion
  539.0 1.3 bitcast_dynamic-update-slice_fusion.7
  540.3 1.7 bitcast_dynamic-update-slice_fusion.6
  542.0 1.7 bitcast_dynamic-update-slice_fusion.5
  543.7 1.7 bitcast_dynamic-update-slice_fusion.4
  545.4 1.7 bitcast_dynamic-update-slice_fusion.3
  547.1 1.7 bitcast_dynamic-update-slice_fusion.2
  548.8 1.7 bitcast_dynamic-update-slice_fusion.1
  550.5 1.8 bitcast_dynamic-update-slice_fusion
  552.3 1.7 bitcast_dynamic-update-slice_fusion.8
  554.0 23.7 %fusion.37 = (bf16[1,9,32,26496]{3,2,1,0:T(8,128)(2,1)}, f32[1,9,32,26496]{3,2,1,0:T(8,128)}) fusion(bf16[9,9,32,32]{3,1,0,2:T(8,128)(2,1)S(1)} %copy-done.3, bf16[9,1,32,26496]{3,2,0,1:T(8,128)(2,1)} %bitcast_dynamic-update-slice_fusion.8), kind=kOutput, calls=%fused_computation.83 | convolution fusion | flops 4402999296 | bytes 61212672 | tf_op jit(solution)/shard_map/dkir,dmix->mkrx/dot_general | solution.py:98
  578.9 1.5 collective-permute-start.2
  580.4 12.4 %copy.120 = bf16[1,384,11520]{1,2,0:T(8,128)(2,1)} copy(bf16[1,384,11520]{2,1,0:T(8,128)(2,1)} %param.13) | data formatting | bytes 17694720 | tf_op args[0]
  592.8 24.6 %slice.209 = f32[1,9,32,25920]{3,2,1,0:T(8,128)} slice(f32[1,9,32,26496]{3,2,1,0:T(8,128)} %get-tuple-element.149), slice={[0:1], [0:9], [0:32], [288:26208]} | slice | bytes 59719680 | tf_op jit(solution)/shard_map/slice | solution.py:103
  617.4 2.3 collective-permute-start.3
  619.7 1.2 slice_add_fusion.1
  621.0 3.7 scatter-add.6
  625.9 3.6 scatter-add.9
  629.5 16.4 %convert_element_type.58 = bf16[1,9,32,25920]{3,2,1,0:T(8,128)(2,1)} convert(f32[1,9,32,25920]{3,2,1,0:T(8,128)} %scatter-add.9) | non-fusion elementwise | flops 7464960 | bytes 44789760 | tf_op jit(solution)/shard_map/convert_element_type | solution.py:106
  646.0 39.3 %reshape.256 = bf16[9,32,360,72]{3,2,1,0:T(8,128)(2,1)} reshape(bf16[1,9,32,25920]{3,2,1,0:T(8,128)(2,1)} %convert_element_type.58) | data formatting | bytes 29859840 | tf_op jit(solution)/shard_map/reshape.104
  685.2 31.7 %copy.119 = bf16[9,72,360,32]{2,3,1,0:T(8,128)(2,1)} copy(bf16[9,72,360,32]{1,2,3,0:T(8,128)(2,1)} %bitcast.186) | data formatting | bytes 29859840 | tf_op jit(solution)/shard_map/mkrjo,mcjr->koc/dot_general | solution.py:112
  716.9 25.9 %copy.121 = bf16[648,360,32]{0,2,1:T(8,128)(2,1)} copy(bf16[648,360,32]{1,2,0:T(8,128)(2,1)} %bitcast.188) | data formatting | bytes 29859840 | tf_op jit(solution)/shard_map/reshape.136
  742.8 14.0 %convolution_bitcast_fusion.10 = f32[648,384]{1,0:T(8,128)} fusion(bf16[648,360,32]{0,2,1:T(8,128)(2,1)} %copy.121, bf16[384,360,32]{0,2,1:T(8,128)(2,1)} %bitcast.189), kind=kOutput, calls=%fused_computation.51 | convolution fusion | flops 5733089280 | bytes 24772608 | tf_op jit(solution)/shard_map/mkrjo,mcjr->koc/dot_general | solution.py:112
  756.9 18.1 %fusion.11 = bf16[1,384,360,32]{1,2,3,0:T(8,128)(2,1)} fusion(bf16[9,32,360,72]{3,2,1,0:T(8,128)(2,1)} %reshape.256, bf16[9,72,384,1]{2,1,3,0:T(8,128)(2,1)S(1)} %bitcast.185), kind=kOutput, calls=%fused_computation.35 | convolution fusion | flops 5737512960 | bytes 24274944 | tf_op jit(solution)/shard_map/koc,mkrjo->mcjr/dot_general | solution.py:107
  775.0 8.2 copy.118
  783.2 12.3 %copy.122 = bf16[1,384,11520]{2,1,0:T(8,128)(2,1)} copy(bf16[1,384,11520]{1,2,0:T(8,128)(2,1)} %bitcast.190) | data formatting | bytes 17694720
  795.5 148.4 %all-gather.5.cloned.1.call-done = f32[20736,384]{1,0:T(8,128)} async-done(((f32[648,384]{1,0:T(8,128)}), f32[20736,384]{1,0:T(8,128)}) %all-gather.5.cloned.1.call-update) | async-done | bytes 31850512 | tf_op jit(solution)/shard_map/all_gather | solution.py:117
  943.9 11.7 %reduce_sum.9 = f32[648,384]{1,0:T(8,128)S(1)} reduce(f32[32,648,384]{2,1,0:T(8,128)} %bitcast.191, f32[]{:T(128)} %constant.97.clone.1), dimensions={0}, to_apply=%region_2.3 | reduce | flops 7713792 | bytes 32845828 | tf_op jit(solution)/shard_map/reduce_sum | solution.py:117
  (30 shorter events, 8.3 us)
Async XLA Ops:
  7.2 31.6 %copy-start = (bf16[648,384]{1,0:T(8,128)(2,1)S(1)}, bf16[648,384]{1,0:T(8,128)(2,1)}, u32[]{:S(2)}) copy-start(bf16[648,384]{1,0:T(8,128)(2,1)} %param.14) | copy-start | bytes 1492996
  7.2 339.2 %all-gather.7.cloned.1.call-start = ((), (), s32[]{:S(2)}) async-start(), calls=%async_computation.1 | async-start | bytes 29859840 | tf_op jit(solution)/shard_map/all_gather | solution.py:83
  8.2 11.1 %collective-permute-start = (bf16[1,384,128]{2,1,0:T(8,128)(2,1)S(1)}, bf16[1,384,128]{2,1,0:T(8,128)(2,1)S(1)}, u32[]{:S(2)}, u32[]{:S(2)}) collective-permute-start(bf16[1,384,128]{2,1,0:T(8,128)(2,1)S(1)} %get-tuple-element.137), channel_id=1, source_target_pairs={{0,1},{1,2},{2,3},{3,0},{4,5},{5,6},{6,7},{7,4},{8,9},{9,10},{10,1... | collective-permute-start | bytes 294920 | tf_op jit(solution)/shard_map/ppermute | solution.py:21
  11.3 8.0 collective-permute-start.1
  17.4 1.0 copy-start.2
  126.7 9.7 %copy-start.1 = (bf16[1,9,32,26496]{3,2,1,0:T(8,128)(2,1)S(1)}, bf16[1,9,32,26496]{3,2,1,0:T(8,128)(2,1)}, u32[]{:S(2)}) copy-start(bf16[1,9,32,26496]{3,2,1,0:T(8,128)(2,1)} %reshape.242) | copy-start | bytes 45785092
  183.2 12.7 %copy-start.4 = (bf16[9,32,32]{2,0,1:T(8,128)(2,1)S(1)}, bf16[9,32,32]{2,0,1:T(8,128)(2,1)}, u32[]{:S(2)}) copy-start(bf16[9,32,32]{2,0,1:T(8,128)(2,1)} %get-tuple-element.139) | copy-start | bytes 55300
  183.2 12.7 %copy-start.6 = (f32[25920,32]{0,1:T(8,128)S(1)}, f32[25920,32]{0,1:T(8,128)}, u32[]{:S(2)}) copy-start(f32[25920,32]{0,1:T(8,128)} %convolution_bitcast_fusion.1) | copy-start | bytes 9953284
  215.6 728.3 %all-gather.5.cloned.1.call-start = ((), (), s32[]{:S(2)}) async-start(), calls=%async_computation | async-start | bytes 32845824 | tf_op jit(solution)/shard_map/all_gather | solution.py:117
  495.4 41.3 %copy-start.5 = (f32[32]{0:T(128)S(1)}, f32[32]{0:T(128)}, u32[]{:S(2)}) copy-start(f32[32]{0:T(128)} %param.19) | copy-start | bytes 388
  545.4 8.6 copy-start.3
  578.9 40.9 %collective-permute-start.2 = (bf16[1,9,32,288]{3,2,1,0:T(8,128)(2,1)S(1)}, bf16[1,9,32,288]{3,2,1,0:T(8,128)(2,1)S(1)}, u32[]{:S(2)}, u32[]{:S(2)}) collective-permute-start(bf16[1,9,32,288]{3,2,1,0:T(8,128)(2,1)S(1)} %get-tuple-element.136), channel_id=1, source_target_pairs={{0,1},{1,2},{2,3},{3,0},{4,5},{5,6},{6,7},{7,4},{8,9},{9,10},{10,1... | collective-permute-start | bytes 497672 | tf_op jit(solution)/shard_map/ppermute | solution.py:33
  617.4 7.3 collective-permute-start.3
Sparse Core Ops, SparseCore 0:
  215.7 130.6 all-gather.6
  757.0 186.8 all-gather.4
